TPU v7x, 128 devices: a whole 4x4x4 slice. The times are simulated.
128 devices in a mesh: section: 2 (over core), seq: 16 (over z, y), head: 4 (over x).
Axes of the slice: x: 4, y: 4, z: 4, core: 2. Of those that a mesh axis runs over, the one named last changes fastest.
Arguments:
- query_vectors: bfloat16 [2, 2048, 8192], P('section', 'seq', 'head'), may hold values from -400 to 400
- key_vectors: bfloat16 [2, 2048, 8192], P('section', 'seq', 'head'), may hold values from -6 to 6
- value_vectors: bfloat16 [2, 2048, 8192], P('section', 'seq', 'head'), may hold values from -6 to 6
- prior_state: float32 [2, 64, 128, 128], P('section', 'head'), may hold values from -128 to 128
- doc_ids: int32 [2, 2048], P('section', 'seq'), may hold values from 0 to 3, never falling along the last dimension, each value on 1 to 1024 neighbouring positions
- norm_gain: float32 [2, 8192], P('section', 'head'), may hold values from 0.25 to 1.75
- residual: bfloat16 [2, 2048, 6144], P('section', 'head', 'seq'), may hold values from -6 to 6
- out_weight: bfloat16 [2, 8192, 6144], P('section', 'head', 'seq'), may hold values from -0.0625 to 0.0625
- enc_weight: bfloat16 [2, 6144, 32768], P('section', None, ('seq', 'head')), may hold values from -0.078125 to 0.078125
- enc_bias: float32 [2, 32768], P('section', ('seq', 'head')), may hold values from -5 to 5
Outputs:
- handoff: bfloat16 [2, 2048, 6144], P('section', 'head', 'seq')
- monitor: bfloat16 [2, 32, 32768], P('section', None, ('seq', 'head'))
Inputs may be any that keep to these rules, and one draw needn't show every extreme that they name: `doc_ids`: document numbers never fall along a section's tokens, are 0 at its first token and rise by at most 1 from one token to the next; a document has at most 1024 tokens, and one has exactly that many.
All inputs are finite; a program needn't handle non-finite values.
Results may differ from a plain program's by a relative error of at most 0.0039.
Values may be sent and summed in bfloat16 or wider, within the bound.
No kernel may reach another device: no remote copies, remote signals or barrier semaphores. Data moves between devices by JAX's collectives and lax.ppermute only.
A program may use at most 128 MiB of HBM per device.

v0:
```python
import jax
import jax.numpy as jnp
from jax import lax
from jax.sharding import PartitionSpec as P

HD = 128
POOL = 64
HDIM = 8192
epsilon = 1e-06


def entering(part, axis, combine, identity):
    place = lax.axis_index(axis)
    gathered = jax.tree.map(lambda a: lax.all_gather(a, axis), part)
    state = jax.tree.map(lambda a, e: jnp.zeros_like(a) + jnp.asarray(e, a.dtype), part, identity)

    def one(hop, state):
        return combine(
            state, jax.tree.map(lambda a: lax.dynamic_index_in_dim(a, hop, 0, False), gathered)
        )

    return lax.fori_loop(0, place, one, state)


def passed_along(x, axis, by):
    devices = lax.axis_size(axis)
    return lax.ppermute(x, axis, [(i, (i + by) % devices) for i in range(devices)])


def merge_states(first_pair, second_pair):
    first_state, first_doc = first_pair
    second_state, second_doc = second_pair
    top_doc = jnp.maximum(first_doc, second_doc)
    merged = jnp.where(first_doc == top_doc, first_state, 0.0) + jnp.where(
        second_doc == top_doc, second_state, 0.0
    )
    return (merged, top_doc)


def local(
    query_vectors,
    key_vectors,
    value_vectors,
    prior_state,
    doc_ids,
    norm_gain,
    residual,
    out_weight,
    enc_weight,
    enc_bias,
):
    highest = lax.Precision.HIGHEST
    row_count = query_vectors.shape[1]
    local_heads = query_vectors.shape[2] // HD
    queries = query_vectors[0].reshape(row_count, local_heads, HD)
    keys_block = key_vectors[0].reshape(row_count, local_heads, HD)
    values_block = value_vectors[0].reshape(row_count, local_heads, HD)
    doc_index = doc_ids[0]
    doc_float = doc_index.astype(jnp.float32)
    last_doc = doc_float[-1]
    keys_last = jnp.where(
        (doc_index == doc_index[-1])[:, None, None], keys_block, jnp.zeros_like(keys_block)
    )
    summary = jnp.einsum(
        "thd,the->hde", keys_last, values_block, preferred_element_type=jnp.float32
    )
    identity_pair = (jnp.zeros_like(summary), jnp.full((1,), -1.0, jnp.float32))
    earlier_state, earlier_last = entering(
        (summary, last_doc[None]), "seq", merge_states, identity_pair
    )
    earlier_doc = earlier_last[0]
    incoming_state, incoming_doc = merge_states(
        (prior_state[0], jnp.zeros((), jnp.float32)), (earlier_state, earlier_doc)
    )
    inter = jnp.einsum(
        "thd,hde->the", queries.astype(jnp.float32), incoming_state, precision=highest
    )
    inter = inter * (doc_float == incoming_doc).astype(jnp.float32)[:, None, None]
    scores = jnp.einsum("thd,uhd->htu", queries, keys_block, preferred_element_type=jnp.float32)
    positions = jnp.arange(row_count)
    same_doc = (positions[None, :] <= positions[:, None]) & (
        doc_index[:, None] == doc_index[None, :]
    )
    scores = jnp.where(same_doc[None, :, :], scores, 0.0)
    intra = jnp.einsum("htu,uhe->the", scores, values_block.astype(jnp.float32), precision=highest)
    attended = (inter + intra).reshape(row_count, local_heads * HD)
    total_square = lax.psum(jnp.sum(attended * attended, axis=1), "head")
    inverse_rms = lax.rsqrt(total_square / HDIM + epsilon)
    normed = (attended * inverse_rms[:, None] * norm_gain[0]).astype(jnp.bfloat16)
    projection = out_weight[0]
    partial_sums = jnp.dot(
        lax.all_gather(normed, "seq", axis=0, tiled=True),
        projection,
        preferred_element_type=jnp.float32,
    )
    own_rows = residual[0]
    encoder = enc_weight[0]
    latent_width = encoder.shape[1]
    reduced = lax.psum_scatter(partial_sums, "head", scatter_dimension=0, tiled=True)
    layer_out = (own_rows.astype(jnp.float32) + reduced).astype(jnp.bfloat16)
    features = lax.all_gather(layer_out, "head", axis=0, tiled=True)
    pre_scores = jnp.dot(
        lax.all_gather(features, "seq", axis=1, tiled=True),
        encoder,
        preferred_element_type=jnp.float32,
    )
    latent = jax.nn.relu(pre_scores + enc_bias[0])
    pooled = jnp.mean(latent.reshape(-1, POOL, latent_width), axis=1).astype(jnp.bfloat16)
    handoff, monitor = passed_along((layer_out[None], pooled[None]), "section", 1)
    return (handoff, monitor)


def solution(mesh):
    return jax.shard_map(
        local,
        mesh=mesh,
        in_specs=(
            P("section", "seq", "head"),
            P("section", "seq", "head"),
            P("section", "seq", "head"),
            P("section", "head", None, None),
            P("section", "seq"),
            P("section", "head"),
            P("section", "head", "seq"),
            P("section", "head", "seq"),
            P("section", None, ("seq", "head")),
            P("section", ("seq", "head")),
        ),
        out_specs=(P("section", "head", "seq"), P("section", None, ("seq", "head"))),
        check_vma=False,
    )
```

profile of v0, /device:TPU:1, one launch (start us, length us, event | category | flops | bytes accessed | tf_op | source)
XLA Modules:
  0.0 542.9 jit_solution(13562496052584884869)
XLA Ops:
  7.2 1.3 slice.8
  8.6 1.3 broadcast_compare_fusion
  9.9 1.3 copy.23
  11.2 1.3 copy.24
  12.5 1.5 fusion.14
  14.1 1.2 dynamic-slice
  16.0 0.8 slice_dynamic-update-slice_fusion
  16.8 35.9 %all-reduce = f32[16]{0:T(128)S(1)} all-reduce(f32[16]{0:T(128)S(1)} %slice_dynamic-update-slice_fusion), channel_id=2, replica_groups=mesh['section'=2,'seq'=16,'head'=4] {'seq'}, use_global_device_ids=true, to_apply=%add | all-reduce | flops 16 | bytes 128
  52.8 1.1 copy.25
  54.3 2.2 convolution_bitcast_fusion
  56.5 72.5 %all-gather.13.cloned.1.call-done = f32[256,128,128]{2,1,0:T(8,128)} async-done(((f32[16,128,128]{2,1,0:T(8,128)}), f32[256,128,128]{2,1,0:T(8,128)}) %all-gather.13.cloned.1.call-update) | async-done | bytes 16777232 | tf_op jit(solution)/shard_map/all_gather | solution.py:14
  129.1 3.6 multiply_reduce_fusion
  132.7 8.4 %psum.7 = f32[128]{0:T(128)S(1)} all-reduce(f32[128]{0:T(128)S(1)} %get-tuple-element.50), channel_id=1, replica_groups=mesh['section'=2,'seq'=16,'head'=4] {'head'}, use_global_device_ids=true, to_apply=%region_3.4 | all-reduce | flops 128 | bytes 1024 | tf_op jit(solution)/shard_map/psum | solution.py:87
  141.1 2.4 fusion.9
  143.6 128.4 %all-gather.7.cloned.1.call-done = bf16[2048,2048]{0,1:T(8,128)(2,1)} async-done(((bf16[128,2048]{0,1:T(8,128)(2,1)}), bf16[2048,2048]{0,1:T(8,128)(2,1)}) %all-gather.7.cloned.1.call-update) | async-done | bytes 8388624 | tf_op jit(solution)/shard_map/all_gather | solution.py:92
  272.0 8.7 %fusion.4 = f32[2048,384]{1,0:T(8,128)} fusion(bf16[2048,2048]{0,1:T(8,128)(2,1)} %all-gather.7.cloned.1.call-done, bf16[1,2048,384]{2,1,0:T(8,128)(2,1)S(1)} %copy-done), kind=kOutput, calls=%fused_computation.6 | convolution fusion | flops 3221225472 | bytes 13107200 | tf_op jit(solution)/shard_map/dot_general | solution.py:91
  280.7 38.5 %reduce-scatter.2.cloned.1.call-done = f32[512,384]{1,0:T(8,128)} async-done(((f32[2048,384]{1,0:T(8,128)}), f32[512,384]{1,0:T(8,128)}) %reduce-scatter.2.cloned.1.call-update) | async-done | bytes 786448 | tf_op jit(solution)/shard_map/reduce_scatter | solution.py:99
  319.2 1.9 fusion.12
  321.2 26.3 %all-gather.9.cloned.1.call-done = bf16[2048,384]{1,0:T(8,128)(2,1)} async-done(((bf16[512,384]{1,0:T(8,128)(2,1)}), bf16[2048,384]{1,0:T(8,128)(2,1)}) %all-gather.9.cloned.1.call-update) | async-done | bytes 1572880 | tf_op jit(solution)/shard_map/all_gather | solution.py:101
  347.6 0.8 collective-permute-start
  348.3 164.4 %all-gather.11.cloned.1.call-done = bf16[2048,6144]{1,0:T(8,128)(2,1)} async-done(((bf16[2048,384]{1,0:T(8,128)(2,1)}), bf16[2048,6144]{1,0:T(8,128)(2,1)}) %all-gather.11.cloned.1.call-update) | async-done | bytes 25165840 | tf_op jit(solution)/shard_map/all_gather | solution.py:103
  512.7 19.8 %bitcast_reduce_fusion = f32[32,512]{1,0:T(8,128)S(1)} fusion(bf16[2048,6144]{1,0:T(8,128)(2,1)} %all-gather.11.cloned.1.call-done, bf16[1,6144,512]{2,1,0:T(8,128)(2,1)} %param.20, f32[512]{0:T(512)S(1)} %bitcast.80), kind=kOutput, calls=%fused_computation.4 | convolution fusion | flops 12888031232 | bytes 31524864 | tf_op jit(solution)/shard_map/dot_general | solution.py:102
  532.5 1.6 collective-permute-start.1
  534.1 0.9 collective-permute-done.1
  (34 shorter events, 2.8 us)
Async XLA Ops:
  7.2 264.8 %copy-start = (bf16[1,2048,384]{2,1,0:T(8,128)(2,1)S(1)}, bf16[1,2048,384]{2,1,0:T(8,128)(2,1)}, u32[]{:S(2)}) copy-start(bf16[1,2048,384]{2,1,0:T(8,128)(2,1)} %param.19) | copy-start | bytes 4718596
  7.2 46.7 %copy-start.4 = (s32[1,128]{1,0:T(1,128)S(1)}, s32[1,128]{1,0:T(1,128)}, u32[]{:S(2)}) copy-start(s32[1,128]{1,0:T(1,128)} %param.16) | copy-start | bytes 1540
  7.2 121.8 %all-gather.13.cloned.1.call-start = ((), (), s32[]{:S(2)}) async-start(), calls=%async_computation.5 | async-start | bytes 17825792 | tf_op jit(solution)/shard_map/all_gather | solution.py:14
  14.1 257.9 %all-gather.7.cloned.1.call-start = ((), (), s32[]{:S(2)}) async-start(), calls=%async_computation.1 | async-start | bytes 8912896 | tf_op jit(solution)/shard_map/all_gather | solution.py:92
  129.1 12.0 %copy-start.3 = (f32[1,2048]{1,0:T(1,128)S(1)}, f32[1,2048]{1,0:T(1,128)}, u32[]{:S(2)}) copy-start(f32[1,2048]{1,0:T(1,128)} %param.17) | copy-start | bytes 24580
  143.5 175.7 %copy-start.2 = (bf16[1,512,384]{2,1,0:T(8,128)(2,1)S(1)}, bf16[1,512,384]{2,1,0:T(8,128)(2,1)}, u32[]{:S(2)}) copy-start(bf16[1,512,384]{2,1,0:T(8,128)(2,1)} %param.18) | copy-start | bytes 1179652
  143.5 175.6 %reduce-scatter.2.cloned.1.call-start = ((), (), s32[]{:S(2)}) async-start(), calls=%async_computation.2 | async-start | bytes 3932160 | tf_op jit(solution)/shard_map/reduce_scatter | solution.py:99
  280.7 232.0 %copy-start.5 = (f32[1,512]{1,0:T(1,128)S(1)}, f32[1,512]{1,0:T(1,128)}, u32[]{:S(2)}) copy-start(f32[1,512]{1,0:T(1,128)} %param.21) | copy-start | bytes 6148
  280.7 66.8 %all-gather.9.cloned.1.call-start = ((), (), s32[]{:S(2)}) async-start(), calls=%async_computation.3 | async-start | bytes 1966080 | tf_op jit(solution)/shard_map/all_gather | solution.py:101
  321.2 191.5 %all-gather.11.cloned.1.call-start = ((), (), s32[]{:S(2)}) async-start(), calls=%async_computation.4 | async-start | bytes 26738688 | tf_op jit(solution)/shard_map/all_gather | solution.py:103
  347.6 186.6 %collective-permute-start = (bf16[1,512,384]{2,1,0:T(8,128)(2,1)}, bf16[1,512,384]{2,1,0:T(8,128)(2,1)S(1)}, u32[]{:S(2)}, u32[]{:S(2)}) collective-permute-start(bf16[1,512,384]{2,1,0:T(8,128)(2,1)} %bitcast.76), channel_id=1, source_target_pairs={{0,64},{64,0},{1,65},{65,1},{2,66},{66,2},{3,67},{67,3},{4,68},{68... | collective-permute-start | bytes 1179656 | tf_op jit(solution)/shard_map/ppermute | solution.py:27
  512.7 23.7 %copy-start.1 = (bf16[1,2048,384]{2,1,0:T(8,128)(2,1)S(1)}, bf16[1,2048,384]{2,1,0:T(8,128)(2,1)}, u32[]{:S(2)}) copy-start(bf16[1,2048,384]{2,1,0:T(8,128)(2,1)} %param.19) | copy-start | bytes 4718596
  532.5 2.5 collective-permute-start.1
Sparse Core Ops, SparseCore 0:
  14.2 114.7 all-gather.12
  143.7 128.2 all-gather.6
  280.8 38.3 reduce-scatter.1
  321.3 26.1 all-gather.8
  349.5 163.1 all-gather.10
where the time goes:
time: 544 us; the launch traced here: 543 us
  waiting for transfers between devices  431 us (79%)
  blocking collectives  44.3 us (8%)
  matrix products  36.1 us (7%)
  between operations  13.9 us (3%)
  local copies, waits for them, and re-layouts  8.65 us (2%)
  other arithmetic  6.43 us (1%)
    all_gather x1, waiting for transfers between devices, local(): lax.all_gather(features, 'seq', axis=1, tiled=True)  164 us
    all_gather x1, waiting for transfers between devices, local(): lax.all_gather(normed, 'seq', axis=0, tiled=True)  128 us
    all_gather x1, waiting for transfers between devices, entering(): gathered = jax.tree.map(lambda a: lax.all_gather(a, axis), part)  72.5 us
    reduce_scatter x1, waiting for transfers between devices, local(): lax.psum_scatter(partial_sums, 'head', scatter_dimension=0, tiled=True)  38.5 us
    unnamed x1, blocking collectives  35.9 us
    all_gather x1, waiting for transfers between devices, local(): features = lax.all_gather(layer_out, 'head', axis=0, tiled=True)  26.3 us
    dot_general x1, matrix products, local(): jnp.dot(lax.all_gather(features, 'seq', axis=1, tiled=True), encoder, pre...  19.8 us
  transfers between devices with their start and end apart: 7, of which 6 were waited for; matrix products, arithmetic and copies ran while one was open for 5% of the time, Pallas kernels for 0%

commit v1 on v0

--- a/solution.py
+++ b/solution.py
@@ -88,10 +88,43 @@
     inverse_rms = lax.rsqrt(total_square / HDIM + epsilon)
     normed = (attended * inverse_rms[:, None] * norm_gain[0]).astype(jnp.bfloat16)
     projection = out_weight[0]
+
+    def deliver_chains(x_local, row_dim):
+        big = lax.axis_size("seq")
+        d_next = lax.axis_index("seq")
+        plain, v_now, prior = (big, d_next, x_local.shape[row_dim])
+        parts_seen = []
+        for dev_i, h in enumerate(x_local.shape):
+            parts_seen.append(h * plain if dev_i == row_dim else h)
+        reached = jnp.zeros(parts_seen, x_local.dtype)
+        right_arr = lax.dynamic_update_slice_in_dim(reached, x_local, v_now * prior, axis=row_dim)
+        mat_out = s_next = x_local
+        s = 1
+        while s < plain // 2 + 1:
+            chunks = []
+            dev_i = 0
+            while dev_i < plain:
+                chunks.append((dev_i, (dev_i + 1) % plain))
+                dev_i = dev_i + 1
+            mat_out = lax.ppermute(mat_out, axis_name="seq", perm=chunks)
+            right_arr = lax.dynamic_update_slice_in_dim(
+                right_arr, mat_out, (v_now - s) % plain * prior, axis=row_dim
+            )
+            if 2 * s < plain:
+                shelf = []
+                dev_i = 0
+                while dev_i < plain:
+                    shelf.append((dev_i, (dev_i - 1) % plain))
+                    dev_i = dev_i + 1
+                s_next = lax.ppermute(s_next, axis_name="seq", perm=shelf)
+                right_arr = lax.dynamic_update_slice_in_dim(
+                    right_arr, s_next, (v_now + s) % plain * prior, axis=row_dim
+                )
+            s += 1
+        return right_arr
+
     partial_sums = jnp.dot(
-        lax.all_gather(normed, "seq", axis=0, tiled=True),
-        projection,
-        preferred_element_type=jnp.float32,
+        deliver_chains(normed, 0), projection, preferred_element_type=jnp.float32
     )
     own_rows = residual[0]
     encoder = enc_weight[0]

time: 544 us -> 578 us (1.062)
  starting transfers between devices: 2.58 us -> 85.9 us
  waiting for transfers between devices: 431 us -> 359 us
  local copies, waits for them, and re-layouts: 8.65 us -> 31.2 us
    all_gather x1 -> x0, waiting for transfers between devices: 128 us -> none  [local(): lax.all_gather(normed, 'seq', axis=0, tiled=True)]
    ppermute x0 -> x15, starting transfers between devices: none -> 83.4 us  [the longest x7 79.1 us: deliver_chains(): s_next = lax.ppermute(s_next, axis_name='seq', perm=shelf)]
    ppermute x0 -> x15, waiting for transfers between devices: none -> 52.5 us  [the longest x8 49.9 us: deliver_chains(): mat_out = lax.ppermute(mat_out, axis_name='seq', perm=chunks)]
    dynamic_update_slice x0 -> x15, local copies, waits for them, and re-layouts: none -> 17.7 us  [the longest x8 9.25 us: deliver_chains(): lax.dynamic_update_slice_in_dim(right_arr, mat_out, (v_now - s) % plain *...]
  transfers between devices with their start and end apart: 7 -> 21, of which waited for: 6 -> 16; matrix products, arithmetic and copies ran while one was open for 5% -> 8% of each run, Pallas kernels for 0% -> 0%
where the time goes in v1:
time: 578 us; the launch traced here: 576 us
  waiting for transfers between devices  359 us (62%)
  starting transfers between devices  85.9 us (15%)
  blocking collectives  44.4 us (8%)
  matrix products  36.1 us (6%)
  local copies, waits for them, and re-layouts  31.2 us (5%)
  between operations  14.2 us (2%)
  other arithmetic  5.93 us (1%)
    all_gather x1, waiting for transfers between devices, local(): lax.all_gather(features, 'seq', axis=1, tiled=True)  164 us
    ppermute x7, starting transfers between devices, deliver_chains(): s_next = lax.ppermute(s_next, axis_name='seq', perm=shelf)  79.1 us
    all_gather x1, waiting for transfers between devices, entering(): gathered = jax.tree.map(lambda a: lax.all_gather(a, axis), part)  71.7 us
    ppermute x8, waiting for transfers between devices, deliver_chains(): mat_out = lax.ppermute(mat_out, axis_name='seq', perm=chunks)  49.9 us
    reduce_scatter x1, waiting for transfers between devices, local(): lax.psum_scatter(partial_sums, 'head', scatter_dimension=0, tiled=True)  42.5 us
    unnamed x1, blocking collectives  35.9 us
    all_gather x1, waiting for transfers between devices, local(): features = lax.all_gather(layer_out, 'head', axis=0, tiled=True)  26.4 us
    dot_general x1, matrix products, local(): jnp.dot(lax.all_gather(features, 'seq', axis=1, tiled=True), encoder, pre...  19.8 us
  transfers between devices with their start and end apart: 21, of which 16 were waited for; matrix products, arithmetic and copies ran while one was open for 8% of the time, Pallas kernels for 0%

profile of v1, /device:TPU:1, one launch (start us, length us, event | category | flops | bytes accessed | tf_op | source)
XLA Modules:
  0.0 576.3 jit_solution(9147088283656331684)
XLA Ops:
  16.8 35.9 %all-reduce = f32[16]{0:T(128)S(1)} all-reduce(f32[16]{0:T(128)S(1)} %slice_dynamic-update-slice_fusion), channel_id=2, replica_groups=mesh['section'=2,'seq'=16,'head'=4] {'seq'}, use_global_device_ids=true, to_apply=%add | all-reduce | flops 16 | bytes 128
  57.2 71.7 %all-gather.10.cloned.1.call-done = f32[256,128,128]{2,1,0:T(8,128)} async-done(((f32[16,128,128]{2,1,0:T(8,128)}), f32[256,128,128]{2,1,0:T(8,128)}) %all-gather.10.cloned.1.call-update) | async-done | bytes 16777232 | tf_op jit(solution)/shard_map/all_gather | solution.py:14
  129.6 3.6 multiply_reduce_fusion
  133.2 8.5 %psum.7 = f32[128]{0:T(128)S(1)} all-reduce(f32[128]{0:T(128)S(1)} %get-tuple-element.50), channel_id=1, replica_groups=mesh['section'=2,'seq'=16,'head'=4] {'head'}, use_global_device_ids=true, to_apply=%region_3.4 | all-reduce | flops 128 | bytes 1024 | tf_op jit(solution)/shard_map/psum | solution.py:87
  141.7 4.3 broadcast_in_dim.62
  147.2 4.2 collective-permute-start
  151.4 49.9 %collective-permute-start.1 = (bf16[128,2048]{0,1:T(8,128)(2,1)S(1)}, bf16[128,2048]{0,1:T(8,128)(2,1)S(1)}, u32[]{:S(2)}, u32[]{:S(2)}) collective-permute-start(bf16[128,2048]{0,1:T(8,128)(2,1)S(1)} %get-tuple-element.53), channel_id=1, source_target_pairs={{0,60},{4,0},{8,4},{12,8},{16,12},{20,16},{24,20},{28,24},{32,28},... | collective-permute-start | bytes 1572872 | tf_op jit(solution)/shard_map/ppermute | solution.py:119
  201.3 9.5 %collective-permute-done = bf16[128,2048]{0,1:T(8,128)(2,1)S(1)} collective-permute-done((bf16[128,2048]{0,1:T(8,128)(2,1)S(1)}, bf16[128,2048]{0,1:T(8,128)(2,1)S(1)}, u32[]{:S(2)}, u32[]{:S(2)}) %collective-permute-start) | collective-permute-done | bytes 524320 | tf_op jit(solution)/shard_map/ppermute | solution.py:109
  210.9 4.8 collective-permute-start.3
  215.7 8.6 %collective-permute-done.2 = bf16[128,2048]{0,1:T(8,128)(2,1)S(1)} collective-permute-done((bf16[128,2048]{0,1:T(8,128)(2,1)S(1)}, bf16[128,2048]{0,1:T(8,128)(2,1)S(1)}, u32[]{:S(2)}, u32[]{:S(2)}) %collective-permute-start.2) | collective-permute-done | bytes 524320 | tf_op jit(solution)/shard_map/ppermute | solution.py:109
  224.3 4.8 collective-permute-start.5
  229.1 7.8 %collective-permute-done.4 = bf16[128,2048]{0,1:T(8,128)(2,1)} collective-permute-done((bf16[128,2048]{0,1:T(8,128)(2,1)S(1)}, bf16[128,2048]{0,1:T(8,128)(2,1)}, u32[]{:S(2)}, u32[]{:S(2)}) %collective-permute-start.4) | collective-permute-done | bytes 524320 | tf_op jit(solution)/shard_map/ppermute | solution.py:109
  239.1 4.5 collective-permute-start.7
  251.3 4.8 collective-permute-start.9
  262.2 5.2 collective-permute-start.11
  268.3 3.9 collective-permute-done.10
  274.9 5.2 collective-permute-start.13
  281.0 4.7 collective-permute-done.12
  289.5 10.7 %collective-permute-done.14 = bf16[128,2048]{0,1:T(8,128)(2,1)S(1)} collective-permute-done((bf16[128,2048]{0,1:T(8,128)(2,1)S(1)}, bf16[128,2048]{0,1:T(8,128)(2,1)S(1)}, u32[]{:S(2)}, u32[]{:S(2)}) %collective-permute-start.14) | collective-permute-done | bytes 524320 | tf_op jit(solution)/shard_map/ppermute | solution.py:109
  301.2 8.7 %fusion.4 = f32[2048,384]{1,0:T(8,128)} fusion(bf16[2048,2048]{0,1:T(8,128)(2,1)} %constant_dynamic-update-slice_fusion, bf16[1,2048,384]{2,1,0:T(8,128)(2,1)S(1)} %copy-done), kind=kOutput, calls=%fused_computation.6 | convolution fusion | flops 3221225472 | bytes 13107200 | tf_op jit(solution)/shard_map/dot_general | solution.py:126
  310.0 42.5 %reduce-scatter.2.cloned.1.call-done = f32[512,384]{1,0:T(8,128)} async-done(((f32[2048,384]{1,0:T(8,128)}), f32[512,384]{1,0:T(8,128)}) %reduce-scatter.2.cloned.1.call-update) | async-done | bytes 786448 | tf_op jit(solution)/shard_map/reduce_scatter | solution.py:132
  354.5 26.4 %all-gather.6.cloned.1.call-done = bf16[2048,384]{1,0:T(8,128)(2,1)} async-done(((bf16[512,384]{1,0:T(8,128)(2,1)}), bf16[2048,384]{1,0:T(8,128)(2,1)}) %all-gather.6.cloned.1.call-update) | async-done | bytes 1572880 | tf_op jit(solution)/shard_map/all_gather | solution.py:134
  381.7 164.4 %all-gather.8.cloned.1.call-done = bf16[2048,6144]{1,0:T(8,128)(2,1)} async-done(((bf16[2048,384]{1,0:T(8,128)(2,1)}), bf16[2048,6144]{1,0:T(8,128)(2,1)}) %all-gather.8.cloned.1.call-update) | async-done | bytes 25165840 | tf_op jit(solution)/shard_map/all_gather | solution.py:136
  546.1 19.8 %bitcast_reduce_fusion = f32[32,512]{1,0:T(8,128)S(1)} fusion(bf16[2048,6144]{1,0:T(8,128)(2,1)} %all-gather.8.cloned.1.call-done, bf16[1,6144,512]{2,1,0:T(8,128)(2,1)} %param.20, f32[512]{0:T(512)S(1)} %bitcast.80), kind=kOutput, calls=%fused_computation.4 | convolution fusion | flops 12888031232 | bytes 31524864 | tf_op jit(solution)/shard_map/dot_general | solution.py:135
  (83 shorter events, 47.6 us)
Async XLA Ops:
  7.2 294.0 %copy-start = (bf16[1,2048,384]{2,1,0:T(8,128)(2,1)S(1)}, bf16[1,2048,384]{2,1,0:T(8,128)(2,1)}, u32[]{:S(2)}) copy-start(bf16[1,2048,384]{2,1,0:T(8,128)(2,1)} %param.19) | copy-start | bytes 4718596
  7.2 121.7 %all-gather.10.cloned.1.call-start = ((), (), s32[]{:S(2)}) async-start(), calls=%async_computation.4 | async-start | bytes 17825792 | tf_op jit(solution)/shard_map/all_gather | solution.py:14
  14.0 338.5 %reduce-scatter.2.cloned.1.call-start = ((), (), s32[]{:S(2)}) async-start(), calls=%async_computation.1 | async-start | bytes 3932160 | tf_op jit(solution)/shard_map/reduce_scatter | solution.py:132
  147.2 63.7 %collective-permute-start = (bf16[128,2048]{0,1:T(8,128)(2,1)S(1)}, bf16[128,2048]{0,1:T(8,128)(2,1)S(1)}, u32[]{:S(2)}, u32[]{:S(2)}) collective-permute-start(bf16[128,2048]{0,1:T(8,128)(2,1)S(1)} %get-tuple-element.53), channel_id=1, source_target_pairs={{0,4},{4,8},{8,12},{12,16},{16,20},{20,24},{24,28},{28,32},{32,36}... | collective-permute-start | bytes 1572872 | tf_op jit(solution)/shard_map/ppermute | solution.py:109
  151.4 59.4 %collective-permute-start.1 = (bf16[128,2048]{0,1:T(8,128)(2,1)S(1)}, bf16[128,2048]{0,1:T(8,128)(2,1)S(1)}, u32[]{:S(2)}, u32[]{:S(2)}) collective-permute-start(bf16[128,2048]{0,1:T(8,128)(2,1)S(1)} %get-tuple-element.53), channel_id=1, source_target_pairs={{0,60},{4,0},{8,4},{12,8},{16,12},{20,16},{24,20},{28,24},{32,28},... | collective-permute-start | bytes 1572872 | tf_op jit(solution)/shard_map/ppermute | solution.py:119
  210.9 13.4 %collective-permute-start.2 = (bf16[128,2048]{0,1:T(8,128)(2,1)S(1)}, bf16[128,2048]{0,1:T(8,128)(2,1)S(1)}, u32[]{:S(2)}, u32[]{:S(2)}) collective-permute-start(bf16[128,2048]{0,1:T(8,128)(2,1)S(1)} %collective-permute-done), channel_id=1, source_target_pairs={{0,4},{4,8},{8,12},{12,16},{16,20},{20,24},{24,28},{28,32},{32,36}... | collective-permute-start | bytes 1572872 | tf_op jit(solution)/shard_map/ppermute | solution.py:109
  210.9 13.4 %collective-permute-start.3 = (bf16[128,2048]{0,1:T(8,128)(2,1)S(1)}, bf16[128,2048]{0,1:T(8,128)(2,1)}, u32[]{:S(2)}, u32[]{:S(2)}) collective-permute-start(bf16[128,2048]{0,1:T(8,128)(2,1)S(1)} %collective-permute-done.1), channel_id=1, source_target_pairs={{0,60},{4,0},{8,4},{12,8},{16,12},{20,16},{24,20},{28,24},{32,28},... | collective-permute-start | bytes 1572872 | tf_op jit(solution)/shard_map/ppermute | solution.py:119
  224.3 12.6 %collective-permute-start.4 = (bf16[128,2048]{0,1:T(8,128)(2,1)S(1)}, bf16[128,2048]{0,1:T(8,128)(2,1)}, u32[]{:S(2)}, u32[]{:S(2)}) collective-permute-start(bf16[128,2048]{0,1:T(8,128)(2,1)S(1)} %collective-permute-done.2), channel_id=1, source_target_pairs={{0,4},{4,8},{8,12},{12,16},{16,20},{20,24},{24,28},{28,32},{32,36}... | collective-permute-start | bytes 1572872 | tf_op jit(solution)/shard_map/ppermute | solution.py:109
  224.3 14.8 %collective-permute-start.5 = (bf16[128,2048]{0,1:T(8,128)(2,1)}, bf16[128,2048]{0,1:T(8,128)(2,1)S(1)}, u32[]{:S(2)}, u32[]{:S(2)}) collective-permute-start(bf16[128,2048]{0,1:T(8,128)(2,1)} %collective-permute-done.3), channel_id=1, source_target_pairs={{0,60},{4,0},{8,4},{12,8},{16,12},{20,16},{24,20},{28,24},{32,28},... | collective-permute-start | bytes 1572872 | tf_op jit(solution)/shard_map/ppermute | solution.py:119
  236.9 11.6 %collective-permute-start.6 = (bf16[128,2048]{0,1:T(8,128)(2,1)}, bf16[128,2048]{0,1:T(8,128)(2,1)S(1)}, u32[]{:S(2)}, u32[]{:S(2)}) collective-permute-start(bf16[128,2048]{0,1:T(8,128)(2,1)} %collective-permute-done.4), channel_id=1, source_target_pairs={{0,4},{4,8},{8,12},{12,16},{16,20},{20,24},{24,28},{28,32},{32,36}... | collective-permute-start | bytes 1572872 | tf_op jit(solution)/shard_map/ppermute | solution.py:109
  239.1 12.2 %collective-permute-start.7 = (bf16[128,2048]{0,1:T(8,128)(2,1)S(1)}, bf16[128,2048]{0,1:T(8,128)(2,1)S(1)}, u32[]{:S(2)}, u32[]{:S(2)}) collective-permute-start(bf16[128,2048]{0,1:T(8,128)(2,1)S(1)} %collective-permute-done.5), channel_id=1, source_target_pairs={{0,60},{4,0},{8,4},{12,8},{16,12},{20,16},{24,20},{28,24},{32,28},... | collective-permute-start | bytes 1572872 | tf_op jit(solution)/shard_map/ppermute | solution.py:119
  248.4 11.4 %collective-permute-start.8 = (bf16[128,2048]{0,1:T(8,128)(2,1)S(1)}, bf16[128,2048]{0,1:T(8,128)(2,1)S(1)}, u32[]{:S(2)}, u32[]{:S(2)}) collective-permute-start(bf16[128,2048]{0,1:T(8,128)(2,1)S(1)} %collective-permute-done.6), channel_id=1, source_target_pairs={{0,4},{4,8},{8,12},{12,16},{16,20},{20,24},{24,28},{28,32},{32,36}... | collective-permute-start | bytes 1572872 | tf_op jit(solution)/shard_map/ppermute | solution.py:109
  251.3 10.9 %collective-permute-start.9 = (bf16[128,2048]{0,1:T(8,128)(2,1)S(1)}, bf16[128,2048]{0,1:T(8,128)(2,1)S(1)}, u32[]{:S(2)}, u32[]{:S(2)}) collective-permute-start(bf16[128,2048]{0,1:T(8,128)(2,1)S(1)} %collective-permute-done.7), channel_id=1, source_target_pairs={{0,60},{4,0},{8,4},{12,8},{16,12},{20,16},{24,20},{28,24},{32,28},... | collective-permute-start | bytes 1572872 | tf_op jit(solution)/shard_map/ppermute | solution.py:119
  259.8 12.4 %collective-permute-start.10 = (bf16[128,2048]{0,1:T(8,128)(2,1)S(1)}, bf16[128,2048]{0,1:T(8,128)(2,1)S(1)}, u32[]{:S(2)}, u32[]{:S(2)}) collective-permute-start(bf16[128,2048]{0,1:T(8,128)(2,1)S(1)} %collective-permute-done.8), channel_id=1, source_target_pairs={{0,4},{4,8},{8,12},{12,16},{16,20},{20,24},{24,28},{28,32},{32,36}... | collective-permute-start | bytes 1572872 | tf_op jit(solution)/shard_map/ppermute | solution.py:109
  262.2 12.7 %collective-permute-start.11 = (bf16[128,2048]{0,1:T(8,128)(2,1)S(1)}, bf16[128,2048]{0,1:T(8,128)(2,1)S(1)}, u32[]{:S(2)}, u32[]{:S(2)}) collective-permute-start(bf16[128,2048]{0,1:T(8,128)(2,1)S(1)} %collective-permute-done.9), channel_id=1, source_target_pairs={{0,60},{4,0},{8,4},{12,8},{16,12},{20,16},{24,20},{28,24},{32,28},... | collective-permute-start | bytes 1572872 | tf_op jit(solution)/shard_map/ppermute | solution.py:119
  272.2 13.5 %collective-permute-start.12 = (bf16[128,2048]{0,1:T(8,128)(2,1)S(1)}, bf16[128,2048]{0,1:T(8,128)(2,1)S(1)}, u32[]{:S(2)}, u32[]{:S(2)}) collective-permute-start(bf16[128,2048]{0,1:T(8,128)(2,1)S(1)} %collective-permute-done.10), channel_id=1, source_target_pairs={{0,4},{4,8},{8,12},{12,16},{16,20},{20,24},{24,28},{28,32},{32,36}... | collective-permute-start | bytes 1572872 | tf_op jit(solution)/shard_map/ppermute | solution.py:109
  274.9 13.8 %collective-permute-start.13 = (bf16[128,2048]{0,1:T(8,128)(2,1)S(1)}, bf16[128,2048]{0,1:T(8,128)(2,1)S(1)}, u32[]{:S(2)}, u32[]{:S(2)}) collective-permute-start(bf16[128,2048]{0,1:T(8,128)(2,1)S(1)} %collective-permute-done.11), channel_id=1, source_target_pairs={{0,60},{4,0},{8,4},{12,8},{16,12},{20,16},{24,20},{28,24},{32,28},... | collective-permute-start | bytes 1572872 | tf_op jit(solution)/shard_map/ppermute | solution.py:119
  285.7 14.6 %collective-permute-start.14 = (bf16[128,2048]{0,1:T(8,128)(2,1)S(1)}, bf16[128,2048]{0,1:T(8,128)(2,1)S(1)}, u32[]{:S(2)}, u32[]{:S(2)}) collective-permute-start(bf16[128,2048]{0,1:T(8,128)(2,1)S(1)} %collective-permute-done.12), channel_id=1, source_target_pairs={{0,4},{4,8},{8,12},{12,16},{16,20},{20,24},{24,28},{28,32},{32,36}... | collective-permute-start | bytes 1572872 | tf_op jit(solution)/shard_map/ppermute | solution.py:109
  301.2 51.3 %copy-start.5 = (bf16[1,512,384]{2,1,0:T(8,128)(2,1)S(1)}, bf16[1,512,384]{2,1,0:T(8,128)(2,1)}, u32[]{:S(2)}) copy-start(bf16[1,512,384]{2,1,0:T(8,128)(2,1)} %param.18) | copy-start | bytes 1179652
  301.2 244.9 %copy-start.8 = (f32[1,512]{1,0:T(1,128)S(1)}, f32[1,512]{1,0:T(1,128)}, u32[]{:S(2)}) copy-start(f32[1,512]{1,0:T(1,128)} %param.21) | copy-start | bytes 6148
  309.9 71.0 %all-gather.6.cloned.1.call-start = ((), (), s32[]{:S(2)}) async-start(), calls=%async_computation.2 | async-start | bytes 1966080 | tf_op jit(solution)/shard_map/all_gather | solution.py:134
  354.5 191.6 %all-gather.8.cloned.1.call-start = ((), (), s32[]{:S(2)}) async-start(), calls=%async_computation.3 | async-start | bytes 26738688 | tf_op jit(solution)/shard_map/all_gather | solution.py:136
  381.0 186.6 %collective-permute-start.15 = (bf16[1,512,384]{2,1,0:T(8,128)(2,1)}, bf16[1,512,384]{2,1,0:T(8,128)(2,1)S(1)}, u32[]{:S(2)}, u32[]{:S(2)}) collective-permute-start(bf16[1,512,384]{2,1,0:T(8,128)(2,1)} %bitcast.76), channel_id=1, source_target_pairs={{0,64},{64,0},{1,65},{65,1},{2,66},{66,2},{3,67},{67,3},{4,68},{68... | collective-permute-start | bytes 1179656 | tf_op jit(solution)/shard_map/ppermute | solution.py:27
  565.9 2.5 collective-permute-start.16
  (6 other events, 106.2 us)
Sparse Core Ops, SparseCore 0:
  14.1 114.7 all-gather.9
  310.0 42.4 reduce-scatter.1
  354.7 26.1 all-gather.5
  382.9 163.1 all-gather.7
